TPU v7x, 256 devices: a whole 4x4x8 slice. The times are simulated.
256 devices in a mesh: enc: 16 (over z_hi, x), dec: 8 (over y, core), grp: 2 (over z_lo).
Axes of the slice: x: 4, y: 4, z: 8 (z_hi: 4, z_lo: 2; z = z_hi * 2 + z_lo), core: 2. Of those that a mesh axis runs over, the one named last changes fastest.
Arguments:
- images: bfloat16 [256, 4, 32, 1280], P(('enc', 'dec', 'grp')), may hold values from -6 to 6
- ln_gain: float32 [1280], replicated, may hold values from 0.1 to 1.9
- ln_bias: float32 [1280], replicated, may hold values from -3 to 3
- fc1_weight: bfloat16 [5120, 1280], P('enc'), may hold values from -0.15625 to 0.15625
- fc1_bias: float32 [5120], P('enc'), may hold values from -3 to 3
- fc2_weight: bfloat16 [5120, 1280], P('enc'), may hold values from -0.078125 to 0.078125
- fc2_bias: float32 [1280], replicated, may hold values from -3 to 3
- key_weight: bfloat16 [1280, 512], replicated, may hold values from -0.15625 to 0.15625
- value_weight: bfloat16 [1280, 512], replicated, may hold values from -0.15625 to 0.15625
- text: bfloat16 [64, 128, 8192], P(('enc', 'grp')), may hold values from -6 to 6
- query_weight: bfloat16 [8192, 4096], P('enc', 'dec'), may hold values from -0.0625 to 0.0625
- tiles: int32 [16, 8, 2], replicated, may hold values from 1 to 4, as said below
- links: int32 [64, 8], P(('enc', 'grp')), may hold values from 0 to 1, as said below
- lengths: int32 [64], P(('enc', 'grp')), may hold values from 1 to 128
- state_grads: bfloat16 [256, 4, 32, 1280], P(('enc', 'dec', 'grp')), may hold values from -0.125 to 0.125
Outputs:
- context: bfloat16 [64, 128, 4096], P(('enc', 'grp'), None, 'dec')
- fc1_grad: float32 [5120, 1280], P(('enc', 'dec', 'grp'))
- fc2_grad: float32 [5120, 1280], P(('enc', 'dec', 'grp'))
Inputs may be any that keep to these rules, and one draw needn't show every extreme that they name: The 16 images that share their last two indices have 40 tiles together, and one of them has 4. `links`: every text is linked to at least one image.
All inputs are finite; a program needn't handle non-finite values.
Results may differ from a plain program's by a relative error of at most 0.017.
Values may be sent and summed in bfloat16 or wider, within the bound.
No kernel may reach another device: no remote copies, remote signals or barrier semaphores. Data moves between devices by JAX's collectives and lax.ppermute only.
A program may use at most 128 MiB of HBM per device.

v0:
```python
import jax
import jax.numpy as jnp
import numpy as np
from jax import lax
from jax.sharding import PartitionSpec as P

HEADS = 32
KV_HEADS = 4
HD = 128
EPSILON = 1e-06


def laid_out(blocks, dim):
    blocks = jnp.moveaxis(blocks, 0, dim)
    dims = blocks.shape
    return blocks.reshape(*dims[:dim], dims[dim] * dims[dim + 1], *dims[dim + 2 :])


def one_gather(arrays, axis, dims):
    line = jnp.concatenate([a.reshape(-1) for a in arrays])
    lines, at, gathered = (lax.all_gather(line, axis), 0, [])
    for a, dim in zip(arrays, dims):
        blocks = lines[:, at : at + a.size].reshape(-1, *a.shape)
        gathered.append(laid_out(blocks, dim))
        at += a.size
    return tuple(gathered)


def in_blocks(array, dim, size):
    before, after = (array.shape[:dim], array.shape[dim + 1 :])
    return jnp.moveaxis(array.reshape(*before, size, -1, *after), dim, 0)


def summed_on_arrival(array, axis, dim):
    blocks = in_blocks(array, dim, lax.axis_size(axis))
    arrived = lax.all_to_all(blocks, axis, split_axis=0, concat_axis=0, tiled=True)
    return arrived.astype(jnp.float32).sum(axis=0)


def in_one_piece(arrays, axis, dim, along):
    both = jnp.concatenate(arrays, axis=along)
    whole, at, gathered = (summed_on_arrival(both, axis, dim), 0, [])
    for a in arrays:
        gathered.append(lax.slice_in_dim(whole, at, at + a.shape[along], axis=along))
        at += a.shape[along]
    return tuple(gathered)


def normalize_layer(values, gain, shift):
    middle = jnp.mean(values, axis=-1, keepdims=True)
    centered = values - middle
    spread = jnp.mean(centered * centered, axis=-1, keepdims=True)
    return centered * lax.rsqrt(spread + EPSILON) * gain + shift


def normalize_heads(values):
    return values * lax.rsqrt(jnp.mean(values * values, axis=-1, keepdims=True) + EPSILON)


def gelu_slope(values):
    return (
        0.5 * (1.0 + lax.erf(values * 0.7071067811865476))
        + values * jnp.exp(-0.5 * values * values) * 0.3989422804014327
    )


def encoder_rows(rows, fc1_weight, fc1_bias, fc2_weight):
    pre = (
        lax.dot_general(
            rows, fc1_weight, (((1,), (1,)), ((), ())), preferred_element_type=jnp.float32
        )
        + fc1_bias
    )
    hidden = jax.nn.gelu(pre, approximate=False).astype(jnp.bfloat16)
    partial_sum = jnp.dot(hidden, fc2_weight, preferred_element_type=jnp.float32)
    return (pre, hidden, partial_sum)


def weight_terms(rows, pre, hidden, cotangent, fc2_weight):
    hidden_grad = lax.dot_general(
        cotangent, fc2_weight, (((1,), (1,)), ((), ())), preferred_element_type=jnp.float32
    )
    second_term = lax.dot_general(
        hidden, cotangent, (((0,), (0,)), ((), ())), preferred_element_type=jnp.float32
    )
    pre_grad = (hidden_grad * gelu_slope(pre)).astype(jnp.bfloat16)
    first_term = lax.dot_general(
        pre_grad, rows, (((0,), (0,)), ((), ())), preferred_element_type=jnp.float32
    )
    return (first_term, second_term)


def project_heads(states, key_columns, value_columns, heads):
    width = states.shape[-1]
    key_raw = jnp.einsum(
        "rd,dhe->hre",
        states,
        key_columns.reshape(width, heads, HD),
        preferred_element_type=jnp.float32,
    )
    keys = normalize_heads(key_raw).astype(jnp.bfloat16)
    values = jnp.einsum(
        "rd,dhe->hre",
        states,
        value_columns.reshape(width, heads, HD),
        preferred_element_type=jnp.float32,
    ).astype(jnp.bfloat16)
    return (keys, values)


def on_device(
    images,
    ln_gain,
    ln_bias,
    fc1_weight,
    fc1_bias,
    fc2_weight,
    fc2_bias,
    key_weight,
    value_weight,
    text,
    query_weight,
    tiles,
    links,
    lengths,
    state_grads,
):
    dec_count = lax.axis_size("dec")
    enc_place = lax.axis_index("enc")
    dec_place = lax.axis_index("dec")
    grp_place = lax.axis_index("grp")
    slots = images.shape[1]
    patch = images.shape[2]
    width = images.shape[3]
    img_rows = slots * patch
    own_rows = images.reshape(img_rows, width)
    normed = normalize_layer(own_rows.astype(jnp.float32), ln_gain, ln_bias).astype(jnp.bfloat16)
    samples = text.shape[0]
    length = text.shape[1]
    text_rows = text.reshape(samples * length, text.shape[2])
    gathered, query_full = one_gather((normed, query_weight), "enc", (0, 0))
    query_raw = jnp.dot(text_rows, query_full, preferred_element_type=jnp.float32)
    tile_index = jnp.arange(slots)
    pre, hidden, partial_full = encoder_rows(gathered, fc1_weight, fc1_bias, fc2_weight)
    summed = lax.psum_scatter(
        partial_full.astype(jnp.bfloat16), "enc", scatter_dimension=0, tiled=True
    ).astype(jnp.float32)
    states = (own_rows.astype(jnp.float32) + summed + fc2_bias).astype(jnp.bfloat16)
    local_heads = query_weight.shape[1] // HD
    per_group = HEADS // KV_HEADS
    kv_local = max(1, local_heads // per_group)
    key_all, value_all = project_heads(states, key_weight, value_weight, KV_HEADS)
    table = np.array(
        [[peer * local_heads // per_group] for peer in range(dec_count)], np.int32
    ).reshape(-1)
    key_send = jnp.take(key_all, table, axis=0).reshape(dec_count, kv_local, img_rows, HD)
    value_send = jnp.take(value_all, table, axis=0).reshape(dec_count, kv_local, img_rows, HD)
    keys, values = (
        lax.all_to_all(key_send, "dec", split_axis=0, concat_axis=0, tiled=True),
        lax.all_to_all(value_send, "dec", split_axis=0, concat_axis=0, tiled=True),
    )
    heads_each = local_heads // kv_local
    queries = normalize_heads(query_raw.reshape(samples, length, local_heads, HD)).astype(
        jnp.bfloat16
    )
    queries = queries.reshape(samples, length, kv_local, heads_each, HD)
    dec_tiles = tiles[enc_place, :, grp_place]
    live_keys = tile_index[None, :] < dec_tiles[:, None]
    live_keys = jnp.broadcast_to(live_keys[:, :, None], (dec_count, slots, patch)).reshape(
        dec_count, img_rows
    )
    allowed = (links[:, :, None] > 0) & live_keys[None, :, :]
    scores = jnp.einsum(
        "sqghd,jgkd->sghjkq", queries, keys, preferred_element_type=jnp.float32
    ) * HD ** (-0.5)
    weights = jnp.where(allowed[:, None, None, :, :, None], jnp.exp(scores), 0.0)
    totals = jnp.sum(weights, axis=(3, 4), keepdims=True)
    probs = (weights / totals).astype(jnp.bfloat16)
    mixed = jnp.einsum("sghjkq,jgkd->sqghd", probs, values, preferred_element_type=jnp.float32)
    valid = jnp.arange(length)[None, :] < lengths[:, None]
    context = (
        jnp.where(valid[:, :, None, None, None], mixed, 0.0)
        .reshape(samples, length, local_heads * HD)
        .astype(jnp.bfloat16)
    )
    own_tiles = tiles[enc_place, dec_place, grp_place]
    own_live = jnp.broadcast_to((tile_index < own_tiles)[:, None, None], (slots, patch, 1)).reshape(
        img_rows, 1
    )
    cotangent = jnp.where(
        own_live, state_grads.reshape(img_rows, width), jnp.zeros((), state_grads.dtype)
    )
    all_cotangent = lax.all_gather(cotangent, "enc", axis=0, tiled=True)
    first_term, second_term = weight_terms(gathered, pre, hidden, all_cotangent, fc2_weight)
    fc1_grad, fc2_grad = in_one_piece(
        (first_term.astype(jnp.bfloat16), second_term.astype(jnp.bfloat16)), ("dec", "grp"), 0, 1
    )
    return (context, fc1_grad, fc2_grad)


def solution(mesh):
    in_specs = (
        P(("enc", "dec", "grp"), None, None, None),
        P(),
        P(),
        P("enc", None),
        P("enc"),
        P("enc", None),
        P(),
        P(),
        P(),
        P(("enc", "grp"), None, None),
        P("enc", "dec"),
        P(),
        P(("enc", "grp"), None),
        P(("enc", "grp")),
        P(("enc", "dec", "grp"), None, None, None),
    )
    out_specs = (
        P(("enc", "grp"), None, "dec"),
        P(("enc", "dec", "grp"), None),
        P(("enc", "dec", "grp"), None),
    )
    return jax.shard_map(
        on_device, mesh=mesh, in_specs=in_specs, out_specs=out_specs, check_vma=False
    )
```

profile of v0, /device:TPU:1, one launch (start us, length us, event | category | flops | bytes accessed | tf_op | source)
XLA Modules:
  0.0 430.2 jit_solution(6207940955061156679)
XLA Ops:
  7.2 1.2 convert_reduce_fusion.1
  8.4 2.2 reshape.204
  10.6 1.2 multiply_reduce_fusion
  11.8 0.1 div.29
  11.9 2.1 copy.50
  14.2 0.1 rsqrt.28
  14.3 1.0 mul.101
  15.3 1.1 mul.102
  16.4 0.9 sub.16
  17.3 2.0 sub.17
  19.3 1.5 add_convert_fusion
  20.8 1.0 pad_maximum_fusion.1
  21.8 0.0 all-gather.4.cloned.1.call-start
  21.9 0.6 dynamic_slice.7
  22.5 0.6 iota_compare_fusion.2
  23.1 0.1 broadcast_in_dim.79
  23.2 0.1 broadcast_in_dim.80
  23.3 0.8 bitcast_select_fusion.1
  24.2 0.0 reduce-scatter.2.cloned.1.call-start
  24.2 165.6 %all-gather.6.cloned.1.call-done = bf16[6815744]{0:T(1024)(128)(2,1)} async-done(((bf16[425984]{0:T(1024)(128)(2,1)}), bf16[6815744]{0:T(1024)(128)(2,1)}) %all-gather.6.cloned.1.call-update) | async-done | bytes 13631504 | tf_op jit(solution)/shard_map/all_gather | solution.py:21
  189.8 17.3 %reshape.221 = bf16[16,425984]{1,0:T(8,128)(2,1)} reshape(bf16[6815744]{0:T(1024)(128)(2,1)} %all-gather.6.cloned.1.call-done) | data formatting | bytes 27262976 | tf_op jit(solution)/shard_map/all_gather | solution.py:21
  207.1 4.4 %slice.20 = bf16[16,163840]{1,0:T(8,128)(2,1)} slice(bf16[16,425984]{1,0:T(8,128)(2,1)} %reshape.221), slice={[0:16], [0:163840]} | slice | bytes 10485760 | tf_op jit(solution)/shard_map/slice | solution.py:23
  211.5 5.7 %reshape_reshape.6 = bf16[2048,1280]{1,0:T(8,128)(2,1)} reshape(bf16[16,163840]{1,0:T(8,128)(2,1)} %slice.20) | data formatting | bytes 10485760 | tf_op jit(solution)/shard_map/reshape;reshape | solution.py:16
  217.2 10.3 %fusion.4 = (bf16[2048,320]{0,1:T(8,128)(2,1)S(1)}, f32[2048,320]{0,1:T(8,128)}) fusion(f32[320]{0:T(512)S(1)} %copy-done.10, bf16[2048,1280]{1,0:T(8,128)(2,1)} %reshape_reshape.6, bf16[320,1280]{1,0:T(8,128)(2,1)S(1)} %copy-done.8), kind=kOutput, calls=%fused_computation.16 | convolution fusion | flops 1720975360 | bytes 9995520 | tf_op jit(solution)/shard_map/dot_general | solution.py:69
  227.5 1.1 copy-done.14
  228.6 4.7 %convolution_convert_fusion = bf16[2048,1280]{1,0:T(8,128)(2,1)} fusion(bf16[2048,320]{0,1:T(8,128)(2,1)S(1)} %get-tuple-element.15, bf16[320,1280]{1,0:T(8,128)(2,1)S(1)} %copy-done.9), kind=kOutput, calls=%fused_computation.2 | convolution fusion | flops 1680343040 | bytes 7372800 | tf_op jit(solution)/shard_map/dot_general | solution.py:75
  233.3 51.3 %all-gather.4.cloned.1.call-done = bf16[2048,1280]{1,0:T(8,128)(2,1)} async-done(((bf16[128,1280]{1,0:T(8,128)(2,1)}), bf16[2048,1280]{1,0:T(8,128)(2,1)}) %all-gather.4.cloned.1.call-update) | async-done | bytes 5242896 | tf_op jit(solution)/shard_map/all_gather | solution.py:193
  284.6 5.7 %convolution_convert_fusion.1 = bf16[320,1280]{1,0:T(8,128)(2,1)} fusion(bf16[2048,320]{0,1:T(8,128)(2,1)} %copy-done.14, bf16[2048,1280]{1,0:T(8,128)(2,1)} %all-gather.4.cloned.1.call-done), kind=kOutput, calls=%fused_computation.12 | convolution fusion | flops 1678131200 | bytes 7372800 | tf_op jit(solution)/shard_map/dot_general | solution.py:83
  290.3 9.4 %convolution_convert_fusion.2 = bf16[320,1280]{1,0:T(8,128)(2,1)} fusion(bf16[2048,1280]{1,0:T(8,128)(2,1)} %reshape_reshape.6, bf16[2048,1280]{1,0:T(8,128)(2,1)} %all-gather.4.cloned.1.call-done, bf16[320,1280]{1,0:T(8,128)(2,1)S(1)} %copy-done.9, f32[2048,320]{0,1:T(8,128)} %get-tuple-element.16), kind=kOutput, calls=%fused_computation.13 | convolution fusion | flops 3362406400 | bytes 14745600 | tf_op jit(solution)/shard_map/dot_general | solution.py:87
  299.7 1.5 pad_maximum_fusion
  301.2 1.5 reshape.202
  302.7 5.7 %all-to-all-start.2 = ((bf16[16,20,2560]{2,1,0:T(8,128)(2,1)}), bf16[16,20,2560]{2,1,0:T(8,128)(2,1)S(1)}, u32[]{:S(2)}, u32[]{:S(2)}) async-start(bf16[16,20,2560]{2,1,0:T(8,128)(2,1)} %reshape.202), calls=%async_computation.3 | async-start | bytes 3932160 | tf_op jit(solution)/shard_map/all_to_all | solution.py:36
  308.3 0.3 dynamic-slice_reduce_fusion
  308.6 0.1 iota_compare_fusion
  308.7 0.1 broadcast_in_dim.48
  308.8 0.1 and.27
  308.9 0.1 copy.38
  309.0 0.6 iota_compare_fusion.1
  309.6 0.1 broadcast_and_fusion
  309.7 7.2 %slice.21 = bf16[16,262144]{1,0:T(8,128)(2,1)} slice(bf16[16,425984]{1,0:T(8,128)(2,1)} %reshape.221), slice={[0:16], [163840:425984]} | slice | bytes 16777216 | tf_op jit(solution)/shard_map/slice | solution.py:23
  316.9 8.0 %reshape_reshape.7 = bf16[8192,512]{1,0:T(8,128)(2,1)} reshape(bf16[16,262144]{1,0:T(8,128)(2,1)} %slice.21) | data formatting | bytes 16777216 | tf_op jit(solution)/shard_map/reshape;reshape | solution.py:16
  324.9 8.1 %fusion.52 = (f32[256,512]{0,1:T(8,128)}, f32[256,512]{0,1:T(8,128)}) fusion(bf16[8192,512]{1,0:T(8,128)(2,1)} %reshape_reshape.7, bf16[256,8192]{1,0:T(8,128)(2,1)} %bitcast.139), kind=kOutput, calls=%fused_computation.84 | convolution fusion | flops 2147614720 | bytes 13631488 | tf_op jit(solution)/shard_map/dot_general | solution.py:142
  333.0 2.1 mul.114
  335.1 1.2 reduce_sum.57
  336.3 0.1 mul.115
  336.5 1.1 fusion.38
  337.6 0.8 convert_element_type.88
  338.4 1.1 copy.42
  339.5 27.2 %all-to-all-done.2 = bf16[16,20,2560]{2,1,0:T(8,128)(2,1)S(1)} async-done(((bf16[16,20,2560]{2,1,0:T(8,128)(2,1)}), bf16[16,20,2560]{2,1,0:T(8,128)(2,1)S(1)}, u32[]{:S(2)}, u32[]{:S(2)}) %all-to-all-start.2) | async-done | bytes 1638432 | tf_op jit(solution)/shard_map/all_to_all | solution.py:36
  366.7 0.3 convert_reduce_fusion
  367.0 0.7 fusion.51
  367.7 25.6 %reduce-scatter.2.cloned.1.call-done = bf16[128,1280]{1,0:T(8,128)(2,1)} async-done(((bf16[2048,1280]{1,0:T(8,128)(2,1)}), bf16[128,1280]{1,0:T(8,128)(2,1)}) %reduce-scatter.2.cloned.1.call-update) | async-done | bytes 327696 | tf_op jit(solution)/shard_map/reduce_scatter | solution.py:145
  393.4 1.2 fusion.37
  394.6 0.6 multiply_reduce_fusion.1
  395.3 1.3 gather_fusion.1
  396.5 5.9 %all-to-all-start.1 = ((bf16[8,1,128,128]{2,3,1,0:T(8,128)(2,1)}), bf16[8,1,128,128]{2,3,1,0:T(8,128)(2,1)S(1)}, u32[]{:S(2)}, u32[]{:S(2)}) async-start(bf16[8,1,128,128]{2,3,1,0:T(8,128)(2,1)} %bitcast.14), calls=%async_computation.2 | async-start | bytes 524288 | tf_op jit(solution)/shard_map/all_to_all | solution.py:159
  402.4 1.7 fusion.33
  404.1 1.3 gather_fusion
  405.4 3.6 all-to-all-done.1
  408.9 4.4 %all-to-all-start = ((bf16[8,1,128,128]{3,2,1,0:T(8,128)(2,1)}), bf16[8,1,128,128]{3,2,1,0:T(8,128)(2,1)S(1)}, u32[]{:S(2)}, u32[]{:S(2)}) async-start(bf16[8,1,128,128]{3,2,1,0:T(8,128)(2,1)} %bitcast.4), calls=%async_computation.1 | async-start | bytes 524288 | tf_op jit(solution)/shard_map/all_to_all | solution.py:160
  413.3 2.6 fusion
  415.9 3.9 all-to-all-done
  419.8 3.0 fusion.27
  422.8 0.9 copy.44
  (44 shorter events, 0.4 us)
Async XLA Ops:
  7.2 387.4 %copy-start = (bf16[1280,512]{1,0:T(8,128)(2,1)S(1)}, bf16[1280,512]{1,0:T(8,128)(2,1)}, u32[]{:S(2)}) copy-start(bf16[1280,512]{1,0:T(8,128)(2,1)} %param.25) | copy-start | bytes 3932164
  7.2 6.8 %copy-start.4 = (f32[1280]{0:T(1024)S(1)}, f32[1280]{0:T(1024)}, u32[]{:S(2)}) copy-start(f32[1280]{0:T(1024)} %param.20) | copy-start | bytes 15364
  7.2 6.9 %copy-start.5 = (f32[1280]{0:T(1024)S(1)}, f32[1280]{0:T(1024)}, u32[]{:S(2)}) copy-start(f32[1280]{0:T(1024)} %param.19) | copy-start | bytes 15364
  7.2 182.6 %all-gather.6.cloned.1.call-start = ((), (), s32[]{:S(2)}) async-start(), calls=%async_computation.6 | async-start | bytes 14483456 | tf_op jit(solution)/shard_map/all_gather | solution.py:21
  19.3 1.5 copy-start.1
  19.3 2.6 copy-start.6
  20.8 2.5 copy-start.2
  21.8 262.8 %all-gather.4.cloned.1.call-start = ((), (), s32[]{:S(2)}) async-start(), calls=%async_computation.5 | async-start | bytes 5570560 | tf_op jit(solution)/shard_map/all_gather | solution.py:193
  24.2 369.2 %reduce-scatter.2.cloned.1.call-start = ((), (), s32[]{:S(2)}) async-start(), calls=%async_computation.4 | async-start | bytes 5570560 | tf_op jit(solution)/shard_map/reduce_scatter | solution.py:145
  211.4 5.7 %copy-start.8 = (bf16[320,1280]{1,0:T(8,128)(2,1)S(1)}, bf16[320,1280]{1,0:T(8,128)(2,1)}, u32[]{:S(2)}) copy-start(bf16[320,1280]{1,0:T(8,128)(2,1)} %param.21) | copy-start | bytes 2457604
  211.4 5.7 %copy-start.10 = (f32[320]{0:T(512)S(1)}, f32[320]{0:T(512)}, u32[]{:S(2)}) copy-start(f32[320]{0:T(512)} %param.22) | copy-start | bytes 3844
  217.1 11.4 %copy-start.9 = (bf16[320,1280]{1,0:T(8,128)(2,1)S(1)}, bf16[320,1280]{1,0:T(8,128)(2,1)}, u32[]{:S(2)}) copy-start(bf16[320,1280]{1,0:T(8,128)(2,1)} %param.23) | copy-start | bytes 2457604
  227.5 1.1 copy-start.14
  302.7 6.2 %copy-start.11 = (s32[2,8]{1,0:T(2,128)S(1)}, s32[2,8]{1,0:T(2,128)}, u32[]{:S(2)}) copy-start(s32[2,8]{1,0:T(2,128)} %param.30) | copy-start | bytes 196
  302.7 6.3 %copy-start.7 = (s32[8]{0:T(128)S(1)}, s32[8]{0:T(128)}, u32[]{:S(2)}) copy-start(s32[8]{0:T(128)} %constant.140) | copy-start | bytes 100
  302.7 6.3 %copy-start.12 = (s32[2]{0:T(128)S(1)}, s32[2]{0:T(128)}, u32[]{:S(2)}) copy-start(s32[2]{0:T(128)} %param.31) | copy-start | bytes 28
  302.7 64.0 %all-to-all-start.2 = ((bf16[16,20,2560]{2,1,0:T(8,128)(2,1)}), bf16[16,20,2560]{2,1,0:T(8,128)(2,1)S(1)}, u32[]{:S(2)}, u32[]{:S(2)}) async-start(bf16[16,20,2560]{2,1,0:T(8,128)(2,1)} %reshape.202), calls=%async_computation.3 | async-start | bytes 3932160 | tf_op jit(solution)/shard_map/all_to_all | solution.py:36
  336.5 56.9 %copy-start.3 = (f32[1280]{0:T(1024)S(1)}, f32[1280]{0:T(1024)}, u32[]{:S(2)}) copy-start(f32[1280]{0:T(1024)} %param.24) | copy-start | bytes 15364
  396.5 12.4 %all-to-all-start.1 = ((bf16[8,1,128,128]{2,3,1,0:T(8,128)(2,1)}), bf16[8,1,128,128]{2,3,1,0:T(8,128)(2,1)S(1)}, u32[]{:S(2)}, u32[]{:S(2)}) async-start(bf16[8,1,128,128]{2,3,1,0:T(8,128)(2,1)} %bitcast.14), calls=%async_computation.2 | async-start | bytes 524288 | tf_op jit(solution)/shard_map/all_to_all | solution.py:159
  408.9 10.9 %all-to-all-start = ((bf16[8,1,128,128]{3,2,1,0:T(8,128)(2,1)}), bf16[8,1,128,128]{3,2,1,0:T(8,128)(2,1)S(1)}, u32[]{:S(2)}, u32[]{:S(2)}) async-start(bf16[8,1,128,128]{3,2,1,0:T(8,128)(2,1)} %bitcast.4), calls=%async_computation.1 | async-start | bytes 524288 | tf_op jit(solution)/shard_map/all_to_all | solution.py:160
  413.3 6.5 %copy-start.13 = (pred[2,128]{1,0:T(4,128)(4,1)S(1)}, pred[2,128]{1,0:T(4,128)(4,1)}, u32[]{:S(2)}) copy-start(pred[2,128]{1,0:T(4,128)(4,1)} %iota_compare_fusion.1) | copy-start | bytes 772
Sparse Core Ops, SparseCore 0:
  22.0 167.8 all-gather.5
  192.3 92.2 all-gather.3
  288.3 105.0 reduce-scatter.1
where the time goes:
time: 431 us; the launch traced here: 430 us
  waiting for transfers between devices  277 us (64%)
  local copies, waits for them, and re-layouts  64.3 us (15%)
  matrix products  46.2 us (11%)
  starting transfers between devices  16 us (4%)
  between operations  14 us (3%)
  other arithmetic  12.4 us (3%)
    all_gather x1, waiting for transfers between devices, one_gather(): lines, at, gathered = (lax.all_gather(line, axis), 0, [])  166 us
    all_gather x1, waiting for transfers between devices, on_device(): all_cotangent = lax.all_gather(cotangent, 'enc', axis=0, tiled=True)  51.3 us
    all_to_all x1, waiting for transfers between devices, summed_on_arrival(): lax.all_to_all(blocks, axis, split_axis=0, concat_axis=0, tiled=True)  27.2 us
    reduce_scatter x1, waiting for transfers between devices, on_device(): lax.psum_scatter(partial_full.astype(jnp.bfloat16), 'enc', scatter_dimens...  25.6 us
    all_gather x1, local copies, waits for them, and re-layouts, one_gather(): lines, at, gathered = (lax.all_gather(line, axis), 0, [])  17.3 us
    another operation x2, local copies, waits for them, and re-layouts, laid_out(): blocks.reshape(*dims[:dim], dims[dim] * dims[dim + 1], *dims[dim + 2:])  13.7 us
    slice x2, local copies, waits for them, and re-layouts, one_gather(): blocks = lines[:, at:at + a.size].reshape(-1, *a.shape)  11.6 us
    dot_general x1, matrix products, encoder_rows(): lax.dot_general(rows, fc1_weight, (((1,), (1,)), ((), ())), preferred_ele...  10.3 us
  transfers between devices with their start and end apart: 6, of which 6 were waited for; matrix products, arithmetic and copies ran while one was open for 23% of the time, Pallas kernels for 0%

commit v1 on v0

--- a/solution.py
+++ b/solution.py
@@ -125,6 +125,11 @@
     lengths,
     state_grads,
 ):
+
+    def save_the_edges(frame_in):
+        passed = jnp.stack([frame_in for _ in range(lax.axis_size("enc"))])
+        return jnp.concatenate(lax.all_to_all(passed, "enc", 0, 0), 0)
+
     dec_count = lax.axis_size("dec")
     enc_place = lax.axis_index("enc")
     dec_place = lax.axis_index("dec")
@@ -190,7 +195,7 @@
     cotangent = jnp.where(
         own_live, state_grads.reshape(img_rows, width), jnp.zeros((), state_grads.dtype)
     )
-    all_cotangent = lax.all_gather(cotangent, "enc", axis=0, tiled=True)
+    all_cotangent = save_the_edges(cotangent)
     first_term, second_term = weight_terms(gathered, pre, hidden, all_cotangent, fc2_weight)
     fc1_grad, fc2_grad = in_one_piece(
         (first_term.astype(jnp.bfloat16), second_term.astype(jnp.bfloat16)), ("dec", "grp"), 0, 1

time: 431 us -> 481 us (1.12)
  waiting for transfers between devices: 277 us -> 314 us
  starting transfers between devices: 16 us -> 27.2 us
    all_gather x1, waiting for transfers between devices: 166 us -> 256 us  [one_gather(): lines, at, gathered = (lax.all_gather(line, axis), 0, [])]
    all_gather x1 -> x0, waiting for transfers between devices: 51.3 us -> none  [on_device(): all_cotangent = lax.all_gather(cotangent, 'enc', axis=0, tiled=True)]
    all_to_all x0 -> x1, starting transfers between devices: none -> 11.6 us  [save_the_edges(): return jnp.concatenate(lax.all_to_all(passed, 'enc', 0, 0), 0)]
  transfers between devices with their start and end apart: 6 -> 6, of which waited for: 6 -> 5; matrix products, arithmetic and copies ran while one was open for 23% -> 21% of each run, Pallas kernels for 0% -> 0%
where the time goes in v1:
time: 481 us; the launch traced here: 480 us
  waiting for transfers between devices  314 us (65%)
  local copies, waits for them, and re-layouts  67.1 us (14%)
  matrix products  46.3 us (10%)
  starting transfers between devices  27.2 us (6%)
  between operations  14.3 us (3%)
  other arithmetic  11.8 us (2%)
    all_gather x1, waiting for transfers between devices, one_gather(): lines, at, gathered = (lax.all_gather(line, axis), 0, [])  256 us
    all_to_all x1, waiting for transfers between devices, summed_on_arrival(): lax.all_to_all(blocks, axis, split_axis=0, concat_axis=0, tiled=True)  25.9 us
    reduce_scatter x1, waiting for transfers between devices, on_device(): lax.psum_scatter(partial_full.astype(jnp.bfloat16), 'enc', scatter_dimens...  24.6 us
    all_gather x1, local copies, waits for them, and re-layouts, one_gather(): lines, at, gathered = (lax.all_gather(line, axis), 0, [])  17.2 us
    another operation x2, local copies, waits for them, and re-layouts, laid_out(): blocks.reshape(*dims[:dim], dims[dim] * dims[dim + 1], *dims[dim + 2:])  13.7 us
    all_to_all x1, starting transfers between devices, save_the_edges(): return jnp.concatenate(lax.all_to_all(passed, 'enc', 0, 0), 0)  11.6 us
    slice x2, local copies, waits for them, and re-layouts, one_gather(): blocks = lines[:, at:at + a.size].reshape(-1, *a.shape)  11.5 us
    dot_general x1, matrix products, encoder_rows(): lax.dot_general(rows, fc1_weight, (((1,), (1,)), ((), ())), preferred_ele...  10.3 us
  transfers between devices with their start and end apart: 6, of which 5 were waited for; matrix products, arithmetic and copies ran while one was open for 21% of the time, Pallas kernels for 0%

profile of v1, /device:TPU:1, one launch (start us, length us, event | category | flops | bytes accessed | tf_op | source)
XLA Modules:
  0.0 480.3 jit_solution(7580561958040609570)
XLA Ops:
  7.2 1.2 convert_reduce_fusion.1
  8.4 2.2 reshape.217
  10.6 1.2 multiply_reduce_fusion
  11.8 0.1 div.29
  11.9 2.0 copy.50
  14.2 0.1 rsqrt.28
  14.3 1.0 mul.101
  15.3 1.1 mul.102
  16.4 1.0 sub.16
  17.4 2.0 sub.17
  19.4 1.5 add_convert_fusion
  20.9 1.0 pad_maximum_fusion.1
  21.9 0.6 dynamic_slice.7
  22.5 0.6 iota_compare_fusion.2
  23.1 0.1 broadcast_in_dim.79
  23.2 0.1 broadcast_in_dim.80
  23.3 0.1 bitcast_select_fusion.1
  23.4 2.9 stack.2
  26.3 11.6 %all-to-all-start.2 = ((bf16[16,128,1280]{2,1,0:T(8,128)(2,1)}), bf16[16,128,1280]{2,1,0:T(8,128)(2,1)}, u32[]{:S(2)}, u32[]{:S(2)}) async-start(bf16[16,128,1280]{2,1,0:T(8,128)(2,1)} %stack.2), calls=%async_computation.3 | async-start | bytes 10485760 | tf_op jit(solution)/shard_map/all_to_all | solution.py:131
  38.0 0.2 reduce-scatter.2.cloned.1.call-start
  38.2 255.6 %all-gather.3.cloned.1.call-done = bf16[6815744]{0:T(1024)(128)(2,1)} async-done(((bf16[425984]{0:T(1024)(128)(2,1)}), bf16[6815744]{0:T(1024)(128)(2,1)}) %all-gather.3.cloned.1.call-update) | async-done | bytes 13631504 | tf_op jit(solution)/shard_map/all_gather | solution.py:21
  293.8 17.2 %reshape.234 = bf16[16,425984]{1,0:T(8,128)(2,1)} reshape(bf16[6815744]{0:T(1024)(128)(2,1)} %all-gather.3.cloned.1.call-done) | data formatting | bytes 27262976 | tf_op jit(solution)/shard_map/all_gather | solution.py:21
  311.0 4.2 slice.20
  315.2 5.7 %reshape_reshape.6 = bf16[2048,1280]{1,0:T(8,128)(2,1)} reshape(bf16[16,163840]{1,0:T(8,128)(2,1)} %slice.20) | data formatting | bytes 10485760 | tf_op jit(solution)/shard_map/reshape;reshape | solution.py:16
  320.9 10.3 %fusion.4 = (bf16[2048,320]{0,1:T(8,128)(2,1)S(1)}, f32[2048,320]{0,1:T(8,128)}) fusion(f32[320]{0:T(512)S(1)} %copy-done.10, bf16[2048,1280]{1,0:T(8,128)(2,1)} %reshape_reshape.6, bf16[320,1280]{1,0:T(8,128)(2,1)S(1)} %copy-done.8), kind=kOutput, calls=%fused_computation.16 | convolution fusion | flops 1720975360 | bytes 9995520 | tf_op jit(solution)/shard_map/dot_general | solution.py:69
  331.2 1.1 copy-done.14
  332.3 4.7 convolution_convert_fusion
  337.1 5.7 %convolution_convert_fusion.1 = bf16[320,1280]{1,0:T(8,128)(2,1)} fusion(bf16[2048,320]{0,1:T(8,128)(2,1)} %copy-done.14, bf16[2048,1280]{1,0:T(8,128)(2,1)} %bitcast.31), kind=kOutput, calls=%fused_computation.12 | convolution fusion | flops 1678131200 | bytes 7372800 | tf_op jit(solution)/shard_map/dot_general | solution.py:83
  342.8 9.4 %convolution_convert_fusion.2 = bf16[320,1280]{1,0:T(8,128)(2,1)} fusion(bf16[2048,1280]{1,0:T(8,128)(2,1)} %reshape_reshape.6, bf16[2048,1280]{1,0:T(8,128)(2,1)} %bitcast.31, bf16[320,1280]{1,0:T(8,128)(2,1)S(1)} %copy-done.9, f32[2048,320]{0,1:T(8,128)} %get-tuple-element.16), kind=kOutput, calls=%fused_computation.13 | convolution fusion | flops 3362406400 | bytes 14745600 | tf_op jit(solution)/shard_map/dot_general | solution.py:87
  352.2 1.5 pad_maximum_fusion
  353.7 1.5 reshape.215
  355.2 5.2 %all-to-all-start.3 = ((bf16[16,20,2560]{2,1,0:T(8,128)(2,1)}), bf16[16,20,2560]{2,1,0:T(8,128)(2,1)S(1)}, u32[]{:S(2)}, u32[]{:S(2)}) async-start(bf16[16,20,2560]{2,1,0:T(8,128)(2,1)} %reshape.215), calls=%async_computation.4 | async-start | bytes 3932160 | tf_op jit(solution)/shard_map/all_to_all | solution.py:36
  360.4 0.3 dynamic-slice_reduce_fusion
  360.7 0.1 iota_compare_fusion
  360.8 0.1 broadcast_in_dim.48
  360.9 0.1 and.27
  361.0 0.1 copy.38
  361.1 0.6 iota_compare_fusion.1
  361.7 0.1 broadcast_and_fusion
  361.8 7.2 %slice.21 = bf16[16,262144]{1,0:T(8,128)(2,1)} slice(bf16[16,425984]{1,0:T(8,128)(2,1)} %reshape.234), slice={[0:16], [163840:425984]} | slice | bytes 16777216 | tf_op jit(solution)/shard_map/slice | solution.py:23
  369.1 8.0 %reshape_reshape.7 = bf16[8192,512]{1,0:T(8,128)(2,1)} reshape(bf16[16,262144]{1,0:T(8,128)(2,1)} %slice.21) | data formatting | bytes 16777216 | tf_op jit(solution)/shard_map/reshape;reshape | solution.py:16
  377.0 8.2 %fusion.52 = (f32[256,512]{0,1:T(8,128)}, f32[256,512]{0,1:T(8,128)}) fusion(bf16[8192,512]{1,0:T(8,128)(2,1)} %reshape_reshape.7, bf16[256,8192]{1,0:T(8,128)(2,1)} %bitcast.140), kind=kOutput, calls=%fused_computation.84 | convolution fusion | flops 2147614720 | bytes 13631488 | tf_op jit(solution)/shard_map/dot_general | solution.py:147
  385.2 2.1 mul.114
  387.3 1.2 reduce_sum.57
  388.6 0.1 mul.115
  388.7 1.1 fusion.38
  389.8 0.8 convert_element_type.88
  390.6 1.1 copy.42
  391.8 25.9 %all-to-all-done.3 = bf16[16,20,2560]{2,1,0:T(8,128)(2,1)S(1)} async-done(((bf16[16,20,2560]{2,1,0:T(8,128)(2,1)}), bf16[16,20,2560]{2,1,0:T(8,128)(2,1)S(1)}, u32[]{:S(2)}, u32[]{:S(2)}) %all-to-all-start.3) | async-done | bytes 1638432 | tf_op jit(solution)/shard_map/all_to_all | solution.py:36
  417.6 0.3 convert_reduce_fusion
  417.9 0.7 fusion.51
  418.7 24.6 %reduce-scatter.2.cloned.1.call-done = bf16[128,1280]{1,0:T(8,128)(2,1)} async-done(((bf16[2048,1280]{1,0:T(8,128)(2,1)}), bf16[128,1280]{1,0:T(8,128)(2,1)}) %reduce-scatter.2.cloned.1.call-update) | async-done | bytes 327696 | tf_op jit(solution)/shard_map/reduce_scatter | solution.py:150
  443.3 1.2 fusion.37
  444.5 0.6 multiply_reduce_fusion.1
  445.2 1.3 gather_fusion.1
  446.4 5.8 %all-to-all-start.1 = ((bf16[8,1,128,128]{2,3,1,0:T(8,128)(2,1)}), bf16[8,1,128,128]{2,3,1,0:T(8,128)(2,1)S(1)}, u32[]{:S(2)}, u32[]{:S(2)}) async-start(bf16[8,1,128,128]{2,3,1,0:T(8,128)(2,1)} %bitcast.14), calls=%async_computation.2 | async-start | bytes 524288 | tf_op jit(solution)/shard_map/all_to_all | solution.py:164
  452.2 1.7 fusion.33
  453.9 1.3 gather_fusion
  455.1 3.6 all-to-all-done.1
  458.7 4.4 all-to-all-start
  463.1 2.6 fusion
  465.7 3.9 all-to-all-done
  469.6 3.0 fusion.27
  472.6 0.9 copy.44
  (44 shorter events, 0.4 us)
Async XLA Ops:
  7.2 437.3 %copy-start = (bf16[1280,512]{1,0:T(8,128)(2,1)S(1)}, bf16[1280,512]{1,0:T(8,128)(2,1)}, u32[]{:S(2)}) copy-start(bf16[1280,512]{1,0:T(8,128)(2,1)} %param.25) | copy-start | bytes 3932164
  7.2 6.8 %copy-start.4 = (f32[1280]{0:T(1024)S(1)}, f32[1280]{0:T(1024)}, u32[]{:S(2)}) copy-start(f32[1280]{0:T(1024)} %param.20) | copy-start | bytes 15364
  7.2 6.9 %copy-start.5 = (f32[1280]{0:T(1024)S(1)}, f32[1280]{0:T(1024)}, u32[]{:S(2)}) copy-start(f32[1280]{0:T(1024)} %param.19) | copy-start | bytes 15364
  7.2 286.6 %all-gather.3.cloned.1.call-start = ((), (), s32[]{:S(2)}) async-start(), calls=%async_computation.6 | async-start | bytes 14483456 | tf_op jit(solution)/shard_map/all_gather | solution.py:21
  19.4 1.5 copy-start.1
  19.4 2.5 copy-start.6
  20.9 2.5 copy-start.2
  26.3 310.7 %all-to-all-start.2 = ((bf16[16,128,1280]{2,1,0:T(8,128)(2,1)}), bf16[16,128,1280]{2,1,0:T(8,128)(2,1)}, u32[]{:S(2)}, u32[]{:S(2)}) async-start(bf16[16,128,1280]{2,1,0:T(8,128)(2,1)} %stack.2), calls=%async_computation.3 | async-start | bytes 10485760 | tf_op jit(solution)/shard_map/all_to_all | solution.py:131
  38.0 405.3 %reduce-scatter.2.cloned.1.call-start = ((), (), s32[]{:S(2)}) async-start(), calls=%async_computation.5 | async-start | bytes 5570560 | tf_op jit(solution)/shard_map/reduce_scatter | solution.py:150
  315.2 5.7 %copy-start.8 = (bf16[320,1280]{1,0:T(8,128)(2,1)S(1)}, bf16[320,1280]{1,0:T(8,128)(2,1)}, u32[]{:S(2)}) copy-start(bf16[320,1280]{1,0:T(8,128)(2,1)} %param.21) | copy-start | bytes 2457604
  315.2 5.7 %copy-start.10 = (f32[320]{0:T(512)S(1)}, f32[320]{0:T(512)}, u32[]{:S(2)}) copy-start(f32[320]{0:T(512)} %param.22) | copy-start | bytes 3844
  320.9 11.4 %copy-start.9 = (bf16[320,1280]{1,0:T(8,128)(2,1)S(1)}, bf16[320,1280]{1,0:T(8,128)(2,1)}, u32[]{:S(2)}) copy-start(bf16[320,1280]{1,0:T(8,128)(2,1)} %param.23) | copy-start | bytes 2457604
  331.2 1.1 copy-start.14
  355.2 5.8 %copy-start.11 = (s32[2,8]{1,0:T(2,128)S(1)}, s32[2,8]{1,0:T(2,128)}, u32[]{:S(2)}) copy-start(s32[2,8]{1,0:T(2,128)} %param.30) | copy-start | bytes 196
  355.2 5.9 %copy-start.7 = (s32[8]{0:T(128)S(1)}, s32[8]{0:T(128)}, u32[]{:S(2)}) copy-start(s32[8]{0:T(128)} %constant.140) | copy-start | bytes 100
  355.2 5.9 %copy-start.12 = (s32[2]{0:T(128)S(1)}, s32[2]{0:T(128)}, u32[]{:S(2)}) copy-start(s32[2]{0:T(128)} %param.31) | copy-start | bytes 28
  355.2 62.5 %all-to-all-start.3 = ((bf16[16,20,2560]{2,1,0:T(8,128)(2,1)}), bf16[16,20,2560]{2,1,0:T(8,128)(2,1)S(1)}, u32[]{:S(2)}, u32[]{:S(2)}) async-start(bf16[16,20,2560]{2,1,0:T(8,128)(2,1)} %reshape.215), calls=%async_computation.4 | async-start | bytes 3932160 | tf_op jit(solution)/shard_map/all_to_all | solution.py:36
  388.7 54.6 %copy-start.3 = (f32[1280]{0:T(1024)S(1)}, f32[1280]{0:T(1024)}, u32[]{:S(2)}) copy-start(f32[1280]{0:T(1024)} %param.24) | copy-start | bytes 15364
  446.4 12.3 %all-to-all-start.1 = ((bf16[8,1,128,128]{2,3,1,0:T(8,128)(2,1)}), bf16[8,1,128,128]{2,3,1,0:T(8,128)(2,1)S(1)}, u32[]{:S(2)}, u32[]{:S(2)}) async-start(bf16[8,1,128,128]{2,3,1,0:T(8,128)(2,1)} %bitcast.14), calls=%async_computation.2 | async-start | bytes 524288 | tf_op jit(solution)/shard_map/all_to_all | solution.py:164
  458.7 10.9 %all-to-all-start = ((bf16[8,1,128,128]{3,2,1,0:T(8,128)(2,1)}), bf16[8,1,128,128]{3,2,1,0:T(8,128)(2,1)S(1)}, u32[]{:S(2)}, u32[]{:S(2)}) async-start(bf16[8,1,128,128]{3,2,1,0:T(8,128)(2,1)} %bitcast.4), calls=%async_computation.1 | async-start | bytes 524288 | tf_op jit(solution)/shard_map/all_to_all | solution.py:165
  463.1 6.5 %copy-start.13 = (pred[2,128]{1,0:T(4,128)(4,1)S(1)}, pred[2,128]{1,0:T(4,128)(4,1)}, u32[]{:S(2)}) copy-start(pred[2,128]{1,0:T(4,128)(4,1)} %iota_compare_fusion.1) | copy-start | bytes 772
Sparse Core Ops, SparseCore 0:
  22.0 271.7 all-gather.2
  337.2 106.0 reduce-scatter.1
